TPU v7x, 256 devices: a whole 4x4x8 slice. The times are simulated.
256 devices in a mesh: ctx: 2 (over core), exp: 8 (over z), tp: 16 (over y, x).
Axes of the slice: x: 4, y: 4, z: 8, core: 2. Of those that a mesh axis runs over, the one named last changes fastest.
Arguments:
- conv_in: bfloat16 [8, 256, 4096], P('exp', 'ctx', 'tp'), may hold values from -6 to 6
- gate_in: bfloat16 [8, 256, 4096], P('exp', 'ctx', 'tp'), may hold values from -6 to 6
- residual: bfloat16 [8, 256, 2048], P('exp', 'ctx'), may hold values from -6 to 6
- conv_weight: float32 [4, 4096], P(None, 'tp'), may hold values from -3 to 3
- conv_bias: float32 [4096], P('tp'), may hold values from -3 to 3
- proj_weight: bfloat16 [4096, 288], P('tp'), may hold values from -0.09375 to 0.09375
- step_weight: bfloat16 [256, 4096], P(None, 'tp'), may hold values from -0.375 to 0.375
- step_bias: float32 [4096], P('tp'), may hold values from -6 to -2
- decay_log: float32 [16, 4096], P(None, 'tp'), may hold values from -3 to 2
- skip_gain: float32 [4096], P('tp'), may hold values from 0.5 to 1.5
- out_weight: bfloat16 [4096, 2048], P('tp'), may hold values from -0.09375 to 0.09375
- norm_gain: float32 [2048], replicated, may hold values from 0.5 to 1.5
- expert_ids: int32 [8, 256, 2], P('exp', 'ctx'), may hold values from 0 to 7, all different within a row; in each aligned block of 128 rows (0 to 127, 128 to 255, ..., all dimensions but the last counted through in order) at most 64 rows name the same one
- route_gates: float32 [8, 256, 2], P('exp', 'ctx'), may hold values from 0.2 to 1
- expert_weight: bfloat16 [8, 3, 2048, 14336], P('exp', None, None, ('ctx', 'tp')), may hold values from -0.125 to 0.125
Outputs:
- layer_out: bfloat16 [8, 256, 2048], P('exp', 'ctx', 'tp')
Inputs may be any that keep to these rules, and one draw needn't show every extreme that they name: `expert_ids`: the 2 picks of a token differ. Among the picks of the 128 tokens of one sequence block, no expert is named more than 64 times, and in some block one expert is named exactly 64 times.
All inputs are finite; a program needn't handle non-finite values.
Results may differ from a plain program's by a relative error of at most 0.015.
Values may be sent and summed in bfloat16 or wider, within the bound.
A program may use at most 128 MiB of HBM per device.

v0:
```python
import math
import jax
import jax.numpy as jnp
from jax import lax
from jax.sharding import PartitionSpec as P

D = 2048
STATE = 16
DT_RANK = 256
TOP = 2
CAP = 64


def from_behind(block, axis, distance):
    devices = range(lax.axis_size(axis))
    route = [(i - distance, i) for i in devices if i - distance in devices]
    return lax.ppermute(block, axis, route)


def prefix(value, axis, join, neutral):
    count, mine = (lax.axis_size(axis), lax.axis_index(axis))
    pieces = jax.tree.map(lambda part: lax.all_gather(part, axis), value)
    running = jax.tree.map(
        lambda part, zero: jnp.full_like(part, 0) + jnp.asarray(zero, part.dtype), value, neutral
    )

    def hop(position, running):
        longer = join(running, jax.tree.map(lambda part: part[position], pieces))
        return jax.tree.map(lambda new, old: jnp.where(position < mine, new, old), longer, running)

    return lax.fori_loop(0, count - 1, hop, running)


def chain_pair(earlier, later):
    return (earlier[0] * later[0], later[0] * earlier[1] + later[1])


def body(
    conv_in,
    gate_in,
    residual,
    conv_weight,
    conv_bias,
    proj_weight,
    step_weight,
    step_bias,
    decay_log,
    skip_gain,
    out_weight,
    norm_gain,
    expert_ids,
    route_gates,
    expert_weight,
):
    highest = lax.Precision.HIGHEST
    local_x = conv_in[0]
    token_rows = local_x.shape[0]
    channels = local_x.shape[1]
    tap_count = conv_weight.shape[0]
    before = from_behind(local_x[token_rows - tap_count + 1 :], "ctx", 1)
    extended = jnp.concatenate([before, local_x], axis=0).astype(jnp.float32)
    convolved = conv_bias[None, :] + sum(
        (conv_weight[k][None, :] * extended[k : k + token_rows] for k in range(tap_count))
    )
    xconv = jax.nn.silu(convolved).astype(jnp.bfloat16)
    projected = lax.psum(jnp.dot(xconv, proj_weight, preferred_element_type=jnp.float32), "tp")
    rank_part = projected[:, :DT_RANK].astype(jnp.bfloat16)
    input_map = projected[:, DT_RANK : DT_RANK + STATE]
    output_map = projected[:, DT_RANK + STATE :]
    step_sizes = jax.nn.softplus(
        jnp.dot(rank_part, step_weight, preferred_element_type=jnp.float32) + step_bias
    )
    decay_rates = -jnp.exp(decay_log)
    xfloat = xconv.astype(jnp.float32)
    driven = step_sizes * xfloat
    span = math.gcd(token_rows, 16)
    block_total = token_rows // span

    def run_block(state, pieces):
        steps_here, driven_here, in_here, out_here = pieces
        emitted = []
        for inner_step in range(span):
            state = (
                jnp.exp(steps_here[inner_step][None, :] * decay_rates) * state
                + driven_here[inner_step][None, :] * in_here[inner_step][:, None]
            )
            emitted.append(jnp.sum(out_here[inner_step][:, None] * state, axis=0))
        return (state, jnp.stack(emitted))

    pieces = (
        step_sizes.reshape(block_total, span, channels),
        driven.reshape(block_total, span, channels),
        input_map.reshape(block_total, span, STATE),
        output_map.reshape(block_total, span, STATE),
    )
    last_state, local_out = lax.scan(run_block, jnp.zeros((STATE, channels), jnp.float32), pieces)
    local_out = local_out.reshape(token_rows, channels)
    elapsed = jnp.cumsum(step_sizes, axis=0)
    last_decay = jnp.exp(elapsed[token_rows - 1][None, :] * decay_rates)
    incoming = prefix(
        (last_decay, last_state),
        "ctx",
        chain_pair,
        (jnp.ones_like(last_decay), jnp.zeros_like(last_state)),
    )[1]
    carried = jnp.sum(
        output_map[:, :, None] * jnp.exp(elapsed[:, None, :] * decay_rates[None]) * incoming[None],
        axis=1,
    )
    scanned = local_out + carried + skip_gain * xfloat
    gated = (scanned * jax.nn.silu(gate_in[0].astype(jnp.float32))).astype(jnp.bfloat16)
    partial_out = jnp.dot(gated, out_weight, preferred_element_type=jnp.float32)
    quarter = D // lax.axis_size("tp")
    lane_start = lax.axis_index("tp") * quarter
    expert_count = lax.axis_size("exp")
    picks = expert_ids[0]
    onehot = (picks[:, :, None] == jnp.arange(expert_count, dtype=jnp.int32)).astype(jnp.int32)
    flat_hot = onehot.reshape(token_rows * TOP, expert_count)
    ranks = jnp.cumsum(flat_hot, axis=0) - 1
    within = jnp.sum(ranks * flat_hot, axis=1).reshape(token_rows, TOP)
    places = picks * CAP + within
    table = (places[:, :, None] == jnp.arange(expert_count * CAP, dtype=jnp.int32)).astype(
        jnp.float32
    )
    chooser = jnp.sum(table, axis=1).astype(jnp.bfloat16)
    blender = jnp.sum(table * route_gates[0][:, :, None], axis=1)
    mixed = lax.psum_scatter(partial_out, "tp", scatter_dimension=1, tiled=True)
    own_residual = lax.dynamic_slice_in_dim(residual[0], lane_start, quarter, 1)
    stream = (own_residual.astype(jnp.float32) + mixed).astype(jnp.bfloat16)
    sfloat = stream.astype(jnp.float32)
    squares = lax.psum(jnp.sum(sfloat * sfloat, axis=1), "tp")
    own_gain = lax.dynamic_slice_in_dim(norm_gain, lane_start, quarter, 0)
    normed = (sfloat * lax.rsqrt(squares[:, None] / D + 1e-06) * own_gain).astype(jnp.bfloat16)
    picked = lax.dot_general(
        chooser, normed, (((0,), (0,)), ((), ())), preferred_element_type=jnp.float32
    )
    arrived = lax.all_to_all(
        picked.astype(jnp.bfloat16).reshape(expert_count, CAP, normed.shape[1]),
        "exp",
        split_axis=0,
        concat_axis=0,
        tiled=True,
    )
    arrived = lax.all_gather(arrived, "tp", axis=2, tiled=True)
    slot_rows = arrived.reshape(-1, D)
    local_weights = expert_weight[0]
    piece = lax.all_gather(local_weights, "ctx", axis=2, tiled=True)
    gate_part = jnp.dot(slot_rows, piece[0], preferred_element_type=jnp.float32)
    up_part = jnp.dot(slot_rows, piece[1], preferred_element_type=jnp.float32)
    hidden = (jax.nn.silu(gate_part) * up_part).astype(jnp.bfloat16)
    summed = jnp.zeros((slot_rows.shape[0], D), jnp.float32) + lax.dot_general(
        hidden, piece[2], (((1,), (1,)), ((), ())), preferred_element_type=jnp.float32
    )
    expert_out = (
        lax.psum_scatter(summed, "tp", scatter_dimension=1, tiled=True)
        .astype(jnp.bfloat16)
        .reshape(expert_count, CAP, quarter)
    )
    returned = lax.all_to_all(expert_out, "exp", split_axis=0, concat_axis=0, tiled=True)
    moe = jnp.dot(
        blender,
        returned.reshape(expert_count * CAP, quarter).astype(jnp.float32),
        precision=highest,
        preferred_element_type=jnp.float32,
    )
    final = (sfloat + moe).astype(jnp.bfloat16)
    return final[None]


def solution(mesh):
    placed = (
        P("exp", "ctx", "tp"),
        P("exp", "ctx", "tp"),
        P("exp", "ctx", None),
        P(None, "tp"),
        P("tp"),
        P("tp", None),
        P(None, "tp"),
        P("tp"),
        P(None, "tp"),
        P("tp"),
        P("tp", None),
        P(),
        P("exp", "ctx", None),
        P("exp", "ctx", None),
        P("exp", None, None, ("ctx", "tp")),
    )
    return jax.shard_map(
        body, mesh=mesh, in_specs=placed, out_specs=P("exp", "ctx", "tp"), check_vma=False
    )
```

profile of v0, /device:TPU:2, one launch (start us, length us, event | category | flops | bytes accessed | tf_op | source)
XLA Modules:
  0.0 459.3 jit_solution(14481502077356869707)
XLA Ops:
  6.5 0.8 slice_bitcast_fusion.10
  7.3 1.7 collective-permute-start
  9.1 0.8 fusion.63
  9.9 0.9 maximum_convert_fusion
  10.8 0.8 multiply_convert_fusion.1
  11.6 1.8 fusion.64
  13.4 96.1 %all-reduce.2.cloned.1.call-done = f32[128,288]{0,1:T(8,128)} async-done(((f32[128,288]{0,1:T(8,128)}), f32[128,288]{0,1:T(8,128)}) %all-reduce.2.cloned.1.call-update) | async-done | bytes 147472 | tf_op jit(solution)/shard_map/psum | solution.py:66
  109.5 0.7 fusion.62
  110.4 1.2 convert_multiply_fusion.2
  111.7 0.2 reduce_window_sum.24
  111.9 8.2 %while.3 = (s32[]{:T(128)}, f32[16,256]{1,0:T(8,128)S(1)}, f32[8,16,256]{2,1,0:T(8,128)S(1)}, f32[8,16,256]{2,1,0:T(8,128)S(1)}, f32[16,256]{1,0:T(8,128)S(1)}, ...) while((s32[]{:T(128)}, f32[16,256]{1,0:T(8,128)S(1)}, ...), condition=%wide.region_18.19_spmd.clone, body=%wide.region_1.18_spmd.clone.sunk | while | flops 577554 | bytes 505064 | solution.py:96
  120.2 1.8 all-gather
  122.0 1.8 all-gather.1
  123.8 0.7 multiply_reduce_fusion.16
  124.7 1.3 fusion.65
  126.5 0.6 reduce-window.6
  127.1 0.2 slice_reduce_fusion
  127.7 0.8 dynamic_slice.31
  128.6 76.4 %reduce-scatter.3.cloned.1.call-done = f32[128,128]{1,0:T(8,128)} async-done(((f32[128,2048]{1,0:T(8,128)}), f32[128,128]{1,0:T(8,128)}) %reduce-scatter.3.cloned.1.call-update) | async-done | bytes 65552 | tf_op jit(solution)/shard_map/reduce_scatter | solution.py:127
  205.1 0.9 fusion.50
  206.0 36.3 %psum.15 = f32[128]{0:T(128)S(1)} all-reduce(f32[128]{0:T(128)S(1)} %get-tuple-element.158), channel_id=1, replica_groups=mesh['ctx'=2,'exp'=8,'tp'=16] {'tp'}, use_global_device_ids=true, to_apply=%region_28.29 | all-reduce | flops 128 | bytes 1024 | tf_op jit(solution)/shard_map/psum | solution.py:131
  242.3 0.3 convolution_convert_fusion
  242.6 16.0 %all_to_all.10 = bf16[8,64,128]{2,1,0:T(8,128)(2,1)} all-to-all(bf16[8,64,128]{2,1,0:T(8,128)(2,1)S(1)} %bitcast.278), channel_id=1, replica_groups=mesh['ctx'=2,'exp'=8,'tp'=16] {'exp'}, dimensions={0} | all-to-all | bytes 262144 | tf_op jit(solution)/shard_map/all_to_all | solution.py:137
  258.7 0.5 all-gather.8.cloned.1.call-update
  259.2 44.6 %all-gather.6.cloned.1.call-done = bf16[8,64,2048]{2,1,0:T(8,128)(2,1)} async-done(((bf16[8,64,128]{2,1,0:T(8,128)(2,1)}), bf16[8,64,2048]{2,1,0:T(8,128)(2,1)}) %all-gather.6.cloned.1.call-update) | async-done | bytes 2097168 | tf_op jit(solution)/shard_map/all_gather | solution.py:144
  303.8 29.3 %all-gather.8.cloned.1.call-done = bf16[1,3,2048,896]{2,3,1,0:T(8,128)(2,1)} async-done(((bf16[1,3,2048,448]{2,3,1,0:T(8,128)(2,1)}), bf16[1,3,2048,896]{2,3,1,0:T(8,128)(2,1)}) %all-gather.8.cloned.1.call-update) | async-done | bytes 11010064 | tf_op jit(solution)/shard_map/all_gather | solution.py:147
  333.1 6.3 %fusion.35 = f32[512,896]{1,0:T(8,128)} fusion(bf16[512,2048]{1,0:T(8,128)(2,1)} %bitcast.364, bf16[1,3,2048,896]{2,3,1,0:T(8,128)(2,1)} %all-gather.8.cloned.1.call-done), kind=kOutput, calls=%fused_computation.135 | convolution fusion | flops 1879048192 | bytes 7602176 | tf_op jit(solution)/shard_map/dot_general | solution.py:148
  339.4 10.9 %fusion.33 = f32[512,2048]{1,0:T(8,128)} fusion(bf16[1,3,2048,896]{2,3,1,0:T(8,128)(2,1)} %all-gather.8.cloned.1.call-done, f32[512,896]{1,0:T(8,128)} %fusion.35, bf16[512,2048]{1,0:T(8,128)(2,1)} %bitcast.365), kind=kOutput, calls=%fused_computation.131 | convolution fusion | flops 3760848896 | bytes 15466496 | tf_op jit(solution)/shard_map/dot_general | solution.py:151
  350.4 84.7 %reduce-scatter.5.cloned.1.call-done = f32[512,128]{1,0:T(8,128)} async-done(((f32[512,2048]{1,0:T(8,128)}), f32[512,128]{1,0:T(8,128)}) %reduce-scatter.5.cloned.1.call-update) | async-done | bytes 262160 | tf_op jit(solution)/shard_map/reduce_scatter | solution.py:155
  435.1 1.0 convert_element_type.75
  436.0 15.9 %all_to_all.11 = bf16[8,64,128]{2,1,0:T(8,128)(2,1)S(1)} all-to-all(bf16[8,64,128]{2,1,0:T(8,128)(2,1)S(1)} %bitcast.277), channel_id=1, replica_groups=mesh['ctx'=2,'exp'=8,'tp'=16] {'exp'}, dimensions={0} | all-to-all | bytes 262144 | tf_op jit(solution)/shard_map/all_to_all | solution.py:159
  451.9 0.9 fusion.37
  (124 shorter events, 9.4 us)
Async XLA Ops:
  6.5 118.2 %copy-start = (bf16[256,2048]{1,0:T(8,128)(2,1)S(1)}, bf16[256,2048]{1,0:T(8,128)(2,1)}, u32[]{:S(2)}) copy-start(bf16[256,2048]{1,0:T(8,128)(2,1)} %param.27) | copy-start | bytes 3145732
  6.5 105.3 %copy-start.2 = (f32[16,256]{1,0:T(8,128)S(1)}, f32[16,256]{1,0:T(8,128)}, u32[]{:S(2)}) copy-start(f32[16,256]{1,0:T(8,128)} %param.25) | copy-start | bytes 49156
  6.5 103.0 %all-reduce.2.cloned.1.call-start = ((), (), s32[]{:S(2)}) async-start(), calls=%async_computation.4 | async-start | bytes 294912 | tf_op jit(solution)/shard_map/psum | solution.py:66
  7.3 2.6 collective-permute-start
  13.3 191.7 %reduce-scatter.3.cloned.1.call-start = ((), (), s32[]{:S(2)}) async-start(), calls=%async_computation.5 | async-start | bytes 1114112 | tf_op jit(solution)/shard_map/reduce_scatter | solution.py:127
  111.9 12.7 %copy-start.1 = (bf16[1,128,256]{2,1,0:T(8,128)(2,1)S(1)}, bf16[1,128,256]{2,1,0:T(8,128)(2,1)}, u32[]{:S(2)}) copy-start(bf16[1,128,256]{2,1,0:T(8,128)(2,1)} %param.18) | copy-start | bytes 196612
  111.9 12.6 %copy-start.3 = (f32[256]{0:T(256)S(1)}, f32[256]{0:T(256)}, u32[]{:S(2)}) copy-start(f32[256]{0:T(256)} %param.21) | copy-start | bytes 3076
  111.9 12.6 %copy-start.4 = (f32[256]{0:T(256)S(1)}, f32[256]{0:T(256)}, u32[]{:S(2)}) copy-start(f32[256]{0:T(256)} %param.26) | copy-start | bytes 3076
  124.5 1.6 copy-start.5
  124.7 3.8 copy-start.6
  126.1 177.8 %all-gather.6.cloned.1.call-start = ((), (), s32[]{:S(2)}) async-start(), calls=%async_computation.6 | async-start | bytes 2228224 | tf_op jit(solution)/shard_map/all_gather | solution.py:144
  258.6 74.5 %all-gather.8.cloned.1.call-start = ((), (), s32[]{:S(2)}) async-start(), calls=%async_computation.8 | async-start | bytes 16515072 | tf_op jit(solution)/shard_map/all_gather | solution.py:147
  259.2 175.9 %reduce-scatter.5.cloned.1.call-start = ((), (), s32[]{:S(2)}) async-start(), calls=%async_computation.7 | async-start | bytes 4456448 | tf_op jit(solution)/shard_map/reduce_scatter | solution.py:155
Sparse Core Ops, SparseCore 0:
  13.5 95.9 all-reduce.1
  126.2 78.8 reduce-scatter.2
  258.7 45.0 all-gather.5
  305.5 27.5 all-gather.7
  350.5 84.5 reduce-scatter.4
where the time goes:
time: 460 us; the launch traced here: 459 us
  waiting for transfers between devices  332 us (72%)
  blocking collectives  71.8 us (16%)
  matrix products  22.6 us (5%)
  between operations  13.4 us (3%)
  other arithmetic  10 us (2%)
  local copies, waits for them, and re-layouts  7.51 us (2%)
    psum x1, waiting for transfers between devices, body(): lax.psum(jnp.dot(xconv, proj_weight, preferred_element_type=jnp.float32),...  96.1 us
    reduce_scatter x1, waiting for transfers between devices, body(): lax.psum_scatter(summed, 'tp', scatter_dimension=1, tiled=True)  84.7 us
    reduce_scatter x1, waiting for transfers between devices, body(): mixed = lax.psum_scatter(partial_out, 'tp', scatter_dimension=1, tiled=True)  76.4 us
    all_gather x1, waiting for transfers between devices, body(): arrived = lax.all_gather(arrived, 'tp', axis=2, tiled=True)  44.6 us
    psum x1, blocking collectives, body(): squares = lax.psum(jnp.sum(sfloat * sfloat, axis=1), 'tp')  36.3 us
    all_gather x1, waiting for transfers between devices, body(): piece = lax.all_gather(local_weights, 'ctx', axis=2, tiled=True)  29.3 us
    all_to_all x1, blocking collectives, body(): lax.all_to_all(picked.astype(jnp.bfloat16).reshape(expert_count, CAP, nor...  16 us
    all_to_all x1, blocking collectives, body(): lax.all_to_all(expert_out, 'exp', split_axis=0, concat_axis=0, tiled=True)  15.9 us
  transfers between devices with their start and end apart: 6, of which 5 were waited for; matrix products, arithmetic and copies ran while one was open for 1% of the time, Pallas kernels for 0%

commit v1 on v0

--- a/solution.py
+++ b/solution.py
@@ -63,7 +63,9 @@
         (conv_weight[k][None, :] * extended[k : k + token_rows] for k in range(tap_count))
     )
     xconv = jax.nn.silu(convolved).astype(jnp.bfloat16)
-    projected = lax.psum(jnp.dot(xconv, proj_weight, preferred_element_type=jnp.float32), "tp")
+    part_2 = jnp.dot(xconv, proj_weight, preferred_element_type=jnp.float32)
+    parts = lax.all_gather(part_2, "tp", axis=0, tiled=False)
+    projected = parts.sum(axis=0)
     rank_part = projected[:, :DT_RANK].astype(jnp.bfloat16)
     input_map = projected[:, DT_RANK : DT_RANK + STATE]
     output_map = projected[:, DT_RANK + STATE :]

time: 460 us -> 420 us (0.913)
  waiting for transfers between devices: 332 us -> 291 us
    psum x1 -> x0, waiting for transfers between devices: 96.1 us -> none  [body(): lax.psum(jnp.dot(xconv, proj_weight, preferred_element_type=jnp.float32),...]
    all_gather x0 -> x1, waiting for transfers between devices: none -> 55.9 us  [body(): parts = lax.all_gather(part_2, 'tp', axis=0, tiled=False)]
where the time goes in v1:
time: 420 us
  waiting for transfers between devices  291 us (69%)
  blocking collectives  71.8 us (17%)
  matrix products  21.7 us (5%)
  between operations  13.4 us (3%)
  other arithmetic  10.4 us (2%)
  local copies, waits for them, and re-layouts  9.17 us (2%)
    reduce_scatter x1, waiting for transfers between devices, body(): lax.psum_scatter(summed, 'tp', scatter_dimension=1, tiled=True)  84.6 us
    reduce_scatter x1, waiting for transfers between devices, body(): mixed = lax.psum_scatter(partial_out, 'tp', scatter_dimension=1, tiled=True)  76 us
    all_gather x1, waiting for transfers between devices, body(): parts = lax.all_gather(part_2, 'tp', axis=0, tiled=False)  55.9 us
    all_gather x1, waiting for transfers between devices, body(): arrived = lax.all_gather(arrived, 'tp', axis=2, tiled=True)  44.6 us
    psum x1, blocking collectives, body(): squares = lax.psum(jnp.sum(sfloat * sfloat, axis=1), 'tp')  36.3 us
    all_gather x1, waiting for transfers between devices, body(): piece = lax.all_gather(local_weights, 'ctx', axis=2, tiled=True)  29.3 us
    all_to_all x1, blocking collectives, body(): lax.all_to_all(picked.astype(jnp.bfloat16).reshape(expert_count, CAP, nor...  16 us
    all_to_all x1, blocking collectives, body(): lax.all_to_all(expert_out, 'exp', split_axis=0, concat_axis=0, tiled=True)  15.9 us
  transfers between devices with their start and end apart: 6, of which 5 were waited for; matrix products, arithmetic and copies ran while one was open for 1% of the time, Pallas kernels for 0%

profile of v1, /device:TPU:2, one launch (start us, length us, event | category | flops | bytes accessed | tf_op | source)
XLA Modules:
  0.0 419.8 jit_solution(8504531070430706783)
XLA Ops:
  6.5 0.8 slice_bitcast_fusion.10
  7.3 1.7 collective-permute-start
  9.1 0.8 fusion.63
  9.9 0.9 maximum_convert_fusion
  10.8 0.8 multiply_convert_fusion.1
  11.5 1.8 fusion.64
  13.4 55.9 %all-gather.10.cloned.1.call-done = f32[2048,288]{0,1:T(8,128)} async-done(((f32[128,288]{0,1:T(8,128)}), f32[2048,288]{0,1:T(8,128)}) %all-gather.10.cloned.1.call-update) | async-done | bytes 2359312 | tf_op jit(solution)/shard_map/all_gather | solution.py:67
  69.3 2.1 copy.38
  71.4 0.4 bitcast_reduce_fusion
  72.0 0.3 copy-done.1
  72.3 0.3 convert_multiply_fusion.2
  72.8 8.2 %while.3 = (s32[]{:T(128)}, f32[16,256]{1,0:T(8,128)S(1)}, f32[8,16,256]{2,1,0:T(8,128)S(1)}, f32[8,16,256]{2,1,0:T(8,128)S(1)}, f32[16,256]{1,0:T(8,128)S(1)}, ...) while((s32[]{:T(128)}, f32[16,256]{1,0:T(8,128)S(1)}, ...), condition=%wide.region_18.19_spmd.clone, body=%wide.region_1.18_spmd.clone.sunk | while | flops 577554 | bytes 505064 | solution.py:98
  81.1 1.8 all-gather.1
  82.9 1.8 all-gather.2
  84.7 0.7 multiply_reduce_fusion.16
  85.6 1.3 fusion.65
  87.4 0.6 reduce-window.6
  88.6 0.8 dynamic_slice.31
  89.5 76.0 %reduce-scatter.3.cloned.1.call-done = f32[128,128]{1,0:T(8,128)} async-done(((f32[128,2048]{1,0:T(8,128)}), f32[128,128]{1,0:T(8,128)}) %reduce-scatter.3.cloned.1.call-update) | async-done | bytes 65552 | tf_op jit(solution)/shard_map/reduce_scatter | solution.py:129
  165.6 0.9 fusion.50
  166.5 36.3 %psum.7 = f32[128]{0:T(128)S(1)} all-reduce(f32[128]{0:T(128)S(1)} %get-tuple-element.150), channel_id=1, replica_groups=mesh['ctx'=2,'exp'=8,'tp'=16] {'tp'}, use_global_device_ids=true, to_apply=%region_28.29 | all-reduce | flops 128 | bytes 1024 | tf_op jit(solution)/shard_map/psum | solution.py:133
  202.8 0.3 convolution_convert_fusion
  203.1 16.0 %all_to_all.10 = bf16[8,64,128]{2,1,0:T(8,128)(2,1)} all-to-all(bf16[8,64,128]{2,1,0:T(8,128)(2,1)S(1)} %bitcast.284), channel_id=1, replica_groups=mesh['ctx'=2,'exp'=8,'tp'=16] {'exp'}, dimensions={0} | all-to-all | bytes 262144 | tf_op jit(solution)/shard_map/all_to_all | solution.py:139
  219.1 0.5 all-gather.12.cloned.1.call-update
  219.7 44.6 %all-gather.8.cloned.1.call-done = bf16[8,64,2048]{2,1,0:T(8,128)(2,1)} async-done(((bf16[8,64,128]{2,1,0:T(8,128)(2,1)}), bf16[8,64,2048]{2,1,0:T(8,128)(2,1)}) %all-gather.8.cloned.1.call-update) | async-done | bytes 2097168 | tf_op jit(solution)/shard_map/all_gather | solution.py:146
  264.3 29.3 %all-gather.12.cloned.1.call-done = bf16[1,3,2048,896]{2,3,1,0:T(8,128)(2,1)} async-done(((bf16[1,3,2048,448]{2,3,1,0:T(8,128)(2,1)}), bf16[1,3,2048,896]{2,3,1,0:T(8,128)(2,1)}) %all-gather.12.cloned.1.call-update) | async-done | bytes 11010064 | tf_op jit(solution)/shard_map/all_gather | solution.py:149
  293.6 6.3 %fusion.35 = f32[512,896]{1,0:T(8,128)} fusion(bf16[512,2048]{1,0:T(8,128)(2,1)} %bitcast.370, bf16[1,3,2048,896]{2,3,1,0:T(8,128)(2,1)} %all-gather.12.cloned.1.call-done), kind=kOutput, calls=%fused_computation.135 | convolution fusion | flops 1879048192 | bytes 7602176 | tf_op jit(solution)/shard_map/dot_general | solution.py:150
  299.9 10.9 %fusion.33 = f32[512,2048]{1,0:T(8,128)} fusion(bf16[1,3,2048,896]{2,3,1,0:T(8,128)(2,1)} %all-gather.12.cloned.1.call-done, f32[512,896]{1,0:T(8,128)} %fusion.35, bf16[512,2048]{1,0:T(8,128)(2,1)} %bitcast.371), kind=kOutput, calls=%fused_computation.131 | convolution fusion | flops 3760848896 | bytes 15466496 | tf_op jit(solution)/shard_map/dot_general | solution.py:153
  310.9 84.6 %reduce-scatter.5.cloned.1.call-done = f32[512,128]{1,0:T(8,128)} async-done(((f32[512,2048]{1,0:T(8,128)}), f32[512,128]{1,0:T(8,128)}) %reduce-scatter.5.cloned.1.call-update) | async-done | bytes 262160 | tf_op jit(solution)/shard_map/reduce_scatter | solution.py:157
  395.5 1.0 convert_element_type.75
  396.5 15.9 %all_to_all.11 = bf16[8,64,128]{2,1,0:T(8,128)(2,1)S(1)} all-to-all(bf16[8,64,128]{2,1,0:T(8,128)(2,1)S(1)} %bitcast.283), channel_id=1, replica_groups=mesh['ctx'=2,'exp'=8,'tp'=16] {'exp'}, dimensions={0} | all-to-all | bytes 262144 | tf_op jit(solution)/shard_map/all_to_all | solution.py:161
  412.4 0.9 fusion.37
  (130 shorter events, 9.8 us)
Async XLA Ops:
  6.5 79.1 %copy-start = (bf16[256,2048]{1,0:T(8,128)(2,1)S(1)}, bf16[256,2048]{1,0:T(8,128)(2,1)}, u32[]{:S(2)}) copy-start(bf16[256,2048]{1,0:T(8,128)(2,1)} %param.27) | copy-start | bytes 3145732
  6.5 62.7 %all-gather.10.cloned.1.call-start = ((), (), s32[]{:S(2)}) async-start(), calls=%async_computation.7 | async-start | bytes 2506752 | tf_op jit(solution)/shard_map/all_gather | solution.py:67
  7.3 2.6 collective-permute-start
  13.3 152.3 %reduce-scatter.3.cloned.1.call-start = ((), (), s32[]{:S(2)}) async-start(), calls=%async_computation.4 | async-start | bytes 1114112 | tf_op jit(solution)/shard_map/reduce_scatter | solution.py:129
  71.4 0.9 copy-start.1
  71.4 0.9 copy-start.5
  71.4 1.4 copy-start.3
  72.8 12.6 %copy-start.2 = (bf16[1,128,256]{2,1,0:T(8,128)(2,1)S(1)}, bf16[1,128,256]{2,1,0:T(8,128)(2,1)}, u32[]{:S(2)}) copy-start(bf16[1,128,256]{2,1,0:T(8,128)(2,1)} %param.18) | copy-start | bytes 196612
  72.8 12.6 %copy-start.4 = (f32[256]{0:T(256)S(1)}, f32[256]{0:T(256)}, u32[]{:S(2)}) copy-start(f32[256]{0:T(256)} %param.21) | copy-start | bytes 3076
  72.8 12.6 %copy-start.6 = (f32[256]{0:T(256)S(1)}, f32[256]{0:T(256)}, u32[]{:S(2)}) copy-start(f32[256]{0:T(256)} %param.26) | copy-start | bytes 3076
  85.4 1.6 copy-start.7
  85.6 3.8 copy-start.8
  87.0 177.4 %all-gather.8.cloned.1.call-start = ((), (), s32[]{:S(2)}) async-start(), calls=%async_computation.5 | async-start | bytes 2228224 | tf_op jit(solution)/shard_map/all_gather | solution.py:146
  219.1 74.5 %all-gather.12.cloned.1.call-start = ((), (), s32[]{:S(2)}) async-start(), calls=%async_computation.8 | async-start | bytes 16515072 | tf_op jit(solution)/shard_map/all_gather | solution.py:149
  219.7 175.9 %reduce-scatter.5.cloned.1.call-start = ((), (), s32[]{:S(2)}) async-start(), calls=%async_computation.6 | async-start | bytes 4456448 | tf_op jit(solution)/shard_map/reduce_scatter | solution.py:157
Sparse Core Ops, SparseCore 0:
  13.5 55.7 all-gather.9
  87.1 78.4 reduce-scatter.2
  219.2 45.0 all-gather.7
  266.0 27.5 all-gather.11
  311.0 84.4 reduce-scatter.4
